TPU v7x, 32 devices: a whole 2x2x4 slice. The times are simulated.
32 devices in a mesh: groups: 2 (over y), strip: 4 (over z), cand: 2 (over x), feat: 2 (over core).
Axes of the slice: x: 2, y: 2, z: 4, core: 2. Of those that a mesh axis runs over, the one named last changes fastest.
Arguments:
- src_pos: float32 [3, 32768], P(None, ('groups', 'strip')), parts along dimension 1, may hold values from -1 to 1
- src_feat: bfloat16 [128, 32768], P('feat', ('groups', 'strip')), parts along dimension 1, may hold values from -10.5 to 10.5
- tgt_pos: float32 [3, 32768], P(None, ('groups', 'strip', 'cand')), parts along dimension 1, may hold values from -0.6 to 1.4
- tgt_feat: bfloat16 [128, 32768], P('feat', ('groups', 'strip', 'cand')), parts along dimension 1, may hold values from -10.5 to 10.5
- displacement: float32 [3, 32768], P(None, ('groups', 'strip')), parts along dimension 1, may hold values from -1 to 1
- sigma_sq: float32 [8], P(('groups', 'strip')), parts along dimension 0, may hold values from 0.5 to 2
- seed_target: int32 [32768], P(('groups', 'strip')), parts along dimension 0, may hold values from 0 to 8191
- counts: int32 [8], P(('groups', 'strip')), parts along dimension 0, may hold values from 512 to 4096
- edges: int32 [8, 32768], P(None, ('groups', 'strip')), parts along dimension 1, may hold values from 0 to 12287, as said below
Outputs:
- new_disp: float32 [3, 32768], P(None, ('groups', 'strip')), parts along dimension 1
- match_mass: float32 [32768], P(('groups', 'strip')), parts along dimension 0
There are 2 independent parts, one for each index of `groups`. A program takes and returns all parts, laid end to end along the dimension named above; each array names one. Nothing has to cross between parts.
Inputs may be any that keep to these rules, and one draw needn't show every extreme that they name: `seed_target`: values of 4096 or more mean that the point has no tie point. `edges`: the strip that an edge names exists, and its slot is below that strip's count; for a live source point at slot i the slot that an edge names lies within 16 of i.
All inputs are finite; a program needn't handle non-finite values.
Results may differ from a plain program's by a relative error of at most 0.0003.
Values may be sent and summed in bfloat16 or wider, within the bound.
A program may use at most 128 MiB of HBM per device.

v0:
```python
import math

import jax
import jax.numpy as jnp
from jax import lax
from jax.experimental import pallas as pl
from jax.experimental.pallas import tpu as pltpu
from jax.sharding import PartitionSpec as P

SWEEPS = 4
LANES = 128
BLOCK = 256

feature_scale = 0.18
tie_gain = 3.0
outlier_level = 1.0
strip_offset = 2.0
kernel_scale = 8.0
coherence = 0.1

EXP2 = feature_scale * math.log2(math.e)
FLOOR = outlier_level / feature_scale
MESH = pl.DeviceIdType.MESH


def split3(value):
    high = value.astype(jnp.bfloat16).astype(jnp.float32)
    rest = value - high
    mid = rest.astype(jnp.bfloat16).astype(jnp.float32)
    return high, mid, rest - mid


def rows8(rows, width):
    at = lax.broadcasted_iota(jnp.int32, (8, width), 0)
    out = jnp.zeros((8, width), jnp.float32)
    for i, row in enumerate(rows):
        out = jnp.where(at == i, jnp.broadcast_to(row, (8, width)), out)
    return out


def posterior_kernel(
    sigma_ref, src_feat, tgt_feat, src_pos, disp, tgt_pos, seed, out,
    sfeat, tmat, saug, xmat, send_sem, recv_sem,
):
    chans, points = src_feat.shape
    cands = tgt_feat.shape[1]
    half = points // 2
    me = lax.axis_index("feat")
    other = 1 - me
    offset = lax.axis_index("cand") * cands
    barrier = pltpu.get_barrier_semaphore()
    pl.semaphore_signal(barrier, inc=1, device_id={"feat": other}, device_id_type=MESH)
    pl.semaphore_wait(barrier, 1)
    theirs = pl.ds(pl.multiple_of(other * half, LANES), half)
    mine = pl.ds(pl.multiple_of(me * half, LANES), half)
    copies = [
        pltpu.make_async_remote_copy(
            src_ref=tgt_feat, dst_ref=tmat.at[pl.ds(chans, chans)],
            send_sem=send_sem.at[0], recv_sem=recv_sem.at[0],
            device_id={"feat": other}, device_id_type=MESH,
        ),
        pltpu.make_async_remote_copy(
            src_ref=src_feat.at[:, theirs], dst_ref=sfeat.at[pl.ds(chans, chans)],
            send_sem=send_sem.at[1], recv_sem=recv_sem.at[1],
            device_id={"feat": other}, device_id_type=MESH,
        ),
    ]
    for copy in copies:
        copy.start()
    tmat[0:chans] = tgt_feat[...]
    sfeat[0:chans] = src_feat[:, mine]
    inv = 1.0 / (sigma_ref[0, 0] * feature_scale)
    x = [tgt_pos[i : i + 1, :] for i in range(3)]
    xx = x[0] * x[0] + x[1] * x[1] + x[2] * x[2]
    one = jnp.ones((1, cands), jnp.float32)
    high, mid, low = split3(rows8(x + [xx * (-0.5 * inv), one], cands))
    tmat[2 * chans : 2 * chans + 48] = jnp.concatenate(
        [high, high, mid, mid, high, low], axis=0
    ).astype(jnp.bfloat16)
    high, mid, low = split3(rows8(x + [one], cands))
    columns = jnp.concatenate(
        [high, mid, low, jnp.zeros((LANES - 24, cands), jnp.float32)], axis=0
    )
    xmat[...] = jnp.transpose(columns).astype(jnp.bfloat16)
    z = [src_pos[i : i + 1, mine] + disp[i : i + 1, mine] for i in range(3)]
    zz = z[0] * z[0] + z[1] * z[1] + z[2] * z[2]
    ones = jnp.ones((1, half), jnp.float32)
    high, mid, low = split3(rows8([v * inv for v in z] + [ones, zz * (-0.5 * inv)], half))
    saug[...] = jnp.concatenate([high, mid, high, mid, low, high], axis=0).astype(jnp.bfloat16)
    for copy in copies:
        copy.wait()

    def block(index, carry):
        span = pl.ds(pl.multiple_of(index * BLOCK, BLOCK), BLOCK)
        lhs = jnp.concatenate([sfeat[:, span], saug[:, span]], axis=0)
        score = lax.dot_general(
            lhs, tmat[...], (((0,), (0,)), ((), ())), preferred_element_type=jnp.float32
        )
        seeds = []
        for i in range(BLOCK // LANES):
            row = seed[pl.ds(me * (half // LANES) + index * (BLOCK // LANES) + i, 1), :] - offset
            seeds.append(jnp.transpose(jnp.broadcast_to(row.astype(jnp.float32), (LANES, LANES))))
        seeds = jnp.concatenate(seeds, axis=0)
        lane = lax.broadcasted_iota(jnp.int32, (BLOCK, LANES), 1).astype(jnp.float32)
        pieces = []
        for t in range(cands // LANES):
            piece = score[:, t * LANES : (t + 1) * LANES]
            tie = jnp.where(seeds == lane + float(t * LANES), tie_gain / feature_scale, 0.0)
            pieces.append(piece + tie)
        best = pieces[0]
        for piece in pieces[1:]:
            best = jnp.maximum(best, piece)
        peak = jnp.maximum(jnp.max(best, axis=1, keepdims=True), FLOOR)
        weight = jnp.concatenate([jnp.exp2((piece - peak) * EXP2) for piece in pieces], axis=1)
        high = weight.astype(jnp.bfloat16)
        low = (weight - high.astype(jnp.float32)).astype(jnp.bfloat16)
        sums = jnp.dot(high, xmat[...], preferred_element_type=jnp.float32)
        sums = sums + jnp.dot(low, xmat[...], preferred_element_type=jnp.float32)
        at = lax.broadcasted_iota(jnp.int32, (BLOCK, LANES), 1)
        sums = jnp.where(at == 28, jnp.broadcast_to(peak, (BLOCK, LANES)), sums)
        for i in range(BLOCK // LANES):
            turned = jnp.transpose(sums[i * LANES : (i + 1) * LANES])
            out[index * (BLOCK // LANES) + i] = (
                turned[0:8] + turned[8:16] + turned[16:24] + turned[24:32]
            )
        return carry

    lax.fori_loop(0, half // BLOCK, block, 0)


def sweep_kernel(
    sigma_ref, count_ref, part, src_pos, disp, edges, new_disp, mass_out,
    parts, pos, dis, edge, geo, geo_in, where_at, kern_own, kern_far, field, field_in,
    resid, mass_s, part_send, part_recv, geo_send, geo_recv, field_send, field_recv,
):
    points = src_pos.shape[1]
    tiles = points // LANES
    cand_n, strip_n = lax.axis_size("cand"), lax.axis_size("strip")
    s, c, f = lax.axis_index("strip"), lax.axis_index("cand"), lax.axis_index("feat")
    below, above = s > 0, s < strip_n - 1
    barrier = pltpu.get_barrier_semaphore()
    peers = [(dc, df) for dc in range(cand_n) for df in range(2) if dc or df]

    def peer(dc, df):
        return {"cand": lax.rem(c + dc, cand_n), "feat": lax.rem(f + df, 2)}

    for dc, df in peers:
        pl.semaphore_signal(barrier, inc=1, device_id=peer(dc, df), device_id_type=MESH)

    @pl.when(below)
    def _():
        pl.semaphore_signal(barrier, inc=1, device_id={"strip": s - 1}, device_id_type=MESH)

    @pl.when(above)
    def _():
        pl.semaphore_signal(barrier, inc=1, device_id={"strip": s + 1}, device_id_type=MESH)

    slot = (
        lax.broadcasted_iota(jnp.int32, (tiles, LANES), 0) * LANES
        + lax.broadcasted_iota(jnp.int32, (tiles, LANES), 1)
    )
    live = (slot < count_ref[0, 0]).astype(jnp.float32)
    for t in range(tiles):
        span = slice(t * LANES, (t + 1) * LANES)
        geo[0:3, t, :] = src_pos[:, span]
        dis[:, t, :] = disp[:, span]
        edge[:, t, :] = edges[:, span]
    geo[3] = live
    parts[0, c] = part[...]

    pl.semaphore_wait(barrier, len(peers) + below.astype(jnp.int32) + above.astype(jnp.int32))

    part_copies = []
    for i, (dc, df) in enumerate(peers):
        copy = pltpu.make_async_remote_copy(
            src_ref=part, dst_ref=parts.at[df, c],
            send_sem=part_send.at[i], recv_sem=part_recv.at[i],
            device_id=peer(dc, df), device_id_type=MESH,
        )
        copy.start()
        part_copies.append(copy)

    def beside(src, dst, send, recv):
        down = pltpu.make_async_remote_copy(
            src_ref=src, dst_ref=dst.at[1], send_sem=send.at[0], recv_sem=recv.at[1],
            device_id={"strip": jnp.maximum(s - 1, 0)}, device_id_type=MESH,
        )
        up = pltpu.make_async_remote_copy(
            src_ref=src, dst_ref=dst.at[0], send_sem=send.at[1], recv_sem=recv.at[0],
            device_id={"strip": jnp.minimum(s + 1, strip_n - 1)}, device_id_type=MESH,
        )

        @pl.when(below)
        def _():
            down.start()

        @pl.when(above)
        def _():
            up.start()

        def finish():
            @pl.when(below)
            def _():
                down.wait_send()
                up.wait_recv()

            @pl.when(above)
            def _():
                up.wait_send()
                down.wait_recv()

        return finish

    @pl.when(jnp.logical_not(below))
    def _():
        geo_in[0] = jnp.zeros(geo_in.shape[1:], jnp.float32)
        for k in range(SWEEPS + 1):
            field_in[k, 0] = jnp.zeros(field_in.shape[2:], jnp.float32)

    @pl.when(jnp.logical_not(above))
    def _():
        geo_in[1] = jnp.zeros(geo_in.shape[1:], jnp.float32)
        for k in range(SWEEPS + 1):
            field_in[k, 1] = jnp.zeros(field_in.shape[2:], jnp.float32)

    finish_geo = beside(geo, geo_in, geo_send, geo_recv)
    lane = lax.broadcasted_iota(jnp.int32, (tiles, LANES), 1)
    row = lax.broadcasted_iota(jnp.int32, (tiles, LANES), 0)

    def pair(array):
        ends = jnp.where(lane < LANES // 2, pltpu.roll(array, tiles - 1, 0), pltpu.roll(array, 1, 0))
        return array, ends

    def pick(arrays, at, inside):
        return jnp.where(
            inside,
            jnp.take_along_axis(arrays[0], at, axis=1, mode="promise_in_bounds"),
            jnp.take_along_axis(arrays[1], at, axis=1, mode="promise_in_bounds"),
        )

    def decode(k):
        e = edge[k]
        segment = (e >= points).astype(jnp.int32) + (e >= 2 * points).astype(jnp.int32)
        local = e - segment * points
        return segment, lax.bitwise_and(local, LANES - 1), lax.shift_right_logical(local, 7) == row

    finish_geo()
    sources = [
        [pair(geo_in[0, i]), pair(geo[i]), pair(geo_in[1, i])] for i in range(4)
    ]
    for k in range(edges.shape[0]):
        segment, at, inside = decode(k)
        near = [
            jnp.where(
                segment == 1,
                pick(three[1], at, inside),
                jnp.where(segment == 0, pick(three[0], at, inside), pick(three[2], at, inside)),
            )
            for three in sources
        ]
        d0 = geo[0] - near[0] - strip_offset * (segment - 1).astype(jnp.float32)
        d1 = geo[1] - near[1]
        d2 = geo[2] - near[2]
        squared = d0 * d0 + d1 * d1 + d2 * d2
        value = live * near[3] * jnp.exp(squared * (-0.5 / kernel_scale)) / edges.shape[0]
        value = jnp.where(slot < count_ref[0, 0], value, 0.0)
        kern_own[k] = jnp.where(segment == 1, value, 0.0)
        kern_far[k] = jnp.where(segment == 1, 0.0, value)

    for copy in part_copies:
        copy.wait()
    rows = tiles // 2
    sigma = sigma_ref[0, 0]
    for df in range(2):
        half_at = lax.rem(f + df, 2) * rows
        span = pl.ds(pl.multiple_of(half_at, 8), rows)
        peaks = [parts[df, i, :, 4, :] for i in range(cand_n)]
        peak = peaks[0]
        for other in peaks[1:]:
            peak = jnp.maximum(peak, other)
        sums = [jnp.zeros((rows, LANES), jnp.float32) for _ in range(4)]
        for i in range(cand_n):
            scale = jnp.exp2((peaks[i] - peak) * EXP2)
            sums = [sums[j] + parts[df, i, :, j, :] * scale for j in range(4)]
        denom = sums[3] + jnp.exp2((FLOOR - peak) * EXP2)
        at = lax.broadcasted_iota(jnp.int32, (rows, LANES), 0) * LANES + lax.broadcasted_iota(
            jnp.int32, (rows, LANES), 1
        )
        on = (at + half_at * LANES < count_ref[0, 0]).astype(jnp.float32)
        share = on / denom
        mass = sums[3] * share
        mass_s[span] = mass
        for j in range(3):
            resid[j, span] = sums[j] * share - mass * (geo[j, span] + dis[j, span])

    mass = mass_s[...]
    mass_out[...] = mass
    inverse = 1.0 / (mass + coherence * sigma)
    for j in range(3):
        field[0, j] = resid[j] * inverse

    for step in range(SWEEPS + 1):
        finish = beside(field.at[step], field_in.at[step], field_send.at[step], field_recv.at[step])
        own = [pair(field[step, j]) for j in range(3)]
        acc = [jnp.zeros((tiles, LANES), jnp.float32) for _ in range(3)]
        for k in range(edges.shape[0]):
            _, at, inside = decode(k)
            weight = kern_own[k]
            acc = [acc[j] + weight * pick(own[j], at, inside) for j in range(3)]
        finish()
        low = [pair(field_in[step, 0, j]) for j in range(3)]
        high = [pair(field_in[step, 1, j]) for j in range(3)]
        for k in range(edges.shape[0]):
            segment, at, inside = decode(k)
            weight = kern_far[k]
            acc = [
                acc[j]
                + weight
                * jnp.where(segment == 0, pick(low[j], at, inside), pick(high[j], at, inside))
                for j in range(3)
            ]
        if step < SWEEPS:
            for j in range(3):
                field[step + 1, j] = (resid[j] - mass_s[...] * acc[j]) * inverse
        else:
            for j in range(3):
                pos[j] = dis[j] + field[step, j] + acc[j]
    for t in range(tiles):
        new_disp[:, t * LANES : (t + 1) * LANES] = pos[:, t, :]


def on_device(
    src_pos, src_feat, tgt_pos, tgt_feat, displacement, sigma_sq, seed_target, counts, edges
):
    chans, points = src_feat.shape
    cands = tgt_pos.shape[1]
    half = points // 2
    tiles = points // LANES
    edge_n = edges.shape[0]
    cand_n = lax.axis_size("cand")
    sigma = sigma_sq.reshape(1, 1)
    count = counts.reshape(1, 1)
    vmem = pl.BlockSpec(memory_space=pltpu.VMEM)
    smem = pl.BlockSpec(memory_space=pltpu.SMEM)
    f32, bf16 = jnp.float32, jnp.bfloat16
    part = pl.pallas_call(
        posterior_kernel,
        out_shape=jax.ShapeDtypeStruct((half // LANES, 8, LANES), f32),
        in_specs=[smem] + [vmem] * 6,
        out_specs=vmem,
        scratch_shapes=[
            pltpu.VMEM((2 * chans, half), bf16),
            pltpu.VMEM((2 * chans + 48, cands), bf16),
            pltpu.VMEM((48, half), bf16),
            pltpu.VMEM((cands, LANES), bf16),
            pltpu.SemaphoreType.DMA((2,)),
            pltpu.SemaphoreType.DMA((2,)),
        ],
        compiler_params=pltpu.CompilerParams(
            collective_id=0, has_side_effects=True, vmem_limit_bytes=48 << 20
        ),
    )(sigma, src_feat, tgt_feat, src_pos, displacement, tgt_pos, seed_target.reshape(tiles, LANES))
    grid = (tiles, LANES)
    new_disp, mass = pl.pallas_call(
        sweep_kernel,
        out_shape=(
            jax.ShapeDtypeStruct((3, points), f32),
            jax.ShapeDtypeStruct(grid, f32),
        ),
        in_specs=[smem, smem] + [vmem] * 4,
        out_specs=(vmem, vmem),
        scratch_shapes=[
            pltpu.VMEM((2, cand_n, half // LANES, 8, LANES), f32),
            pltpu.VMEM((3,) + grid, f32),
            pltpu.VMEM((3,) + grid, f32),
            pltpu.VMEM((edge_n,) + grid, jnp.int32),
            pltpu.VMEM((4,) + grid, f32),
            pltpu.VMEM((2, 4) + grid, f32),
            pltpu.VMEM((8, LANES), jnp.int32),
            pltpu.VMEM((edge_n,) + grid, f32),
            pltpu.VMEM((edge_n,) + grid, f32),
            pltpu.VMEM((SWEEPS + 1, 3) + grid, f32),
            pltpu.VMEM((SWEEPS + 1, 2, 3) + grid, f32),
            pltpu.VMEM((3,) + grid, f32),
            pltpu.VMEM(grid, f32),
            pltpu.SemaphoreType.DMA((2 * cand_n - 1,)),
            pltpu.SemaphoreType.DMA((2 * cand_n - 1,)),
            pltpu.SemaphoreType.DMA((2,)),
            pltpu.SemaphoreType.DMA((2,)),
            pltpu.SemaphoreType.DMA((SWEEPS + 1, 2)),
            pltpu.SemaphoreType.DMA((SWEEPS + 1, 2)),
        ],
        compiler_params=pltpu.CompilerParams(
            collective_id=1, has_side_effects=True, vmem_limit_bytes=48 << 20
        ),
    )(sigma, count, part, src_pos, displacement, edges)
    return (new_disp, mass.reshape(points))


def solution(mesh):
    in_specs = (
        P(None, ("groups", "strip")),
        P("feat", ("groups", "strip")),
        P(None, ("groups", "strip", "cand")),
        P("feat", ("groups", "strip", "cand")),
        P(None, ("groups", "strip")),
        P(("groups", "strip")),
        P(("groups", "strip")),
        P(("groups", "strip")),
        P(None, ("groups", "strip")),
    )
    out_specs = (P(None, ("groups", "strip")), P(("groups", "strip")))
    return jax.shard_map(
        on_device, mesh=mesh, in_specs=in_specs, out_specs=out_specs, check_vma=False
    )
```

profile of v0, /device:TPU:0, one launch (start us, length us, event | category | flops | bytes accessed | tf_op | source)
XLA Modules:
  0.0 53.9 jit_solution(2827155626153064087)
XLA Ops:
  1.9 0.0 copy-start
  1.9 1.0 %copy-done = bf16[64,4096]{1,0:T(8,128)(2,1)S(1)} copy-done((bf16[64,4096]{1,0:T(8,128)(2,1)S(1)}, bf16[64,4096]{1,0:T(8,128)(2,1)}, u32[]{:S(2)}) %copy-start) | copy-done | bytes 524312
  3.0 0.0 copy-start.1
  3.0 0.9 %copy-done.1 = bf16[64,2048]{1,0:T(8,128)(2,1)S(1)} copy-done((bf16[64,2048]{1,0:T(8,128)(2,1)S(1)}, bf16[64,2048]{1,0:T(8,128)(2,1)}, u32[]{:S(2)}) %copy-start.1) | copy-done | bytes 262168
  3.9 0.0 copy-start.2
  3.9 0.8 %copy-done.2 = f32[3,4096]{1,0:T(4,128)S(1)} copy-done((f32[3,4096]{1,0:T(4,128)S(1)}, f32[3,4096]{1,0:T(4,128)}, u32[]{:S(2)}) %copy-start.2) | copy-done | bytes 49176
  4.8 0.0 copy-start.3
  4.8 0.8 %copy-done.3 = f32[3,4096]{1,0:T(4,128)S(1)} copy-done((f32[3,4096]{1,0:T(4,128)S(1)}, f32[3,4096]{1,0:T(4,128)}, u32[]{:S(2)}) %copy-start.3) | copy-done | bytes 49176
  5.6 0.0 copy-start.5
  5.6 0.8 %copy-done.5 = f32[3,2048]{1,0:T(4,128)S(1)} copy-done((f32[3,2048]{1,0:T(4,128)S(1)}, f32[3,2048]{1,0:T(4,128)}, u32[]{:S(2)}) %copy-start.5) | copy-done | bytes 24600
  6.4 0.0 copy-start.6
  6.4 0.7 %copy-done.6 = s32[4096]{0:T(1024)S(1)} copy-done((s32[4096]{0:T(1024)S(1)}, s32[4096]{0:T(1024)}, u32[]{:S(2)}) %copy-start.6) | copy-done | bytes 16408
  7.1 0.0 copy-start.4
  7.1 14.1 %shard_map.104.part = f32[16,8,128]{2,1,0:T(8,128)S(1)} custom-call(f32[1,1]{1,0:T(1,128)} %bitcast.4.sigma_ref, bf16[64,4096]{1,0:T(8,128)(2,1)S(1)} %copy-done, bf16[64,2048]{1,0:T(8,128)(2,1)S(1)} %copy-done.1, f32[3,4096]{1,0:T(4,128)S(1)} %copy-done.2, f32[3,4096]{1,0:T(4,128)S(1)} %copy-done.3, f32[3,2048]{1,0:T(4,128)S(1)} %copy-done.5, ...), custom_call_target="tpu_custom_call" | custom-call | tf_op jit(solution)/shard_map/pallas_call | solution.py:346
  21.2 0.0 copy-done.4
  21.2 31.4 %shard_map.105 = (f32[3,4096]{1,0:T(4,128)S(1)}, f32[32,128]{1,0:T(8,128)S(1)}) custom-call(f32[1,1]{1,0:T(1,128)} %bitcast.5.sigma_ref, s32[1,1]{1,0:T(1,128)} %bitcast.6.count_ref, f32[16,8,128]{2,1,0:T(8,128)S(1)} %shard_map.104.part, f32[3,4096]{1,0:T(4,128)S(1)} %copy-done.2, f32[3,4096]{1,0:T(4,128)S(1)} %copy-done.3, s32[8,4096]{1,0:T(8,128)S(1)} %copy-done.4), custom_call_target="tpu_custom_call" | custom-call | tf_op jit(solution)/shard_map/pallas_call | solution.py:364
  52.6 0.6 %copy.15 = f32[3,4096]{1,0:T(4,128)} copy(f32[3,4096]{1,0:T(4,128)S(1)} %get-tuple-element.8) | data formatting | bytes 98304
  53.3 0.6 %copy.16 = f32[4096]{0:T(1024)} copy(f32[4096]{0:T(1024)S(1)} %bitcast.8) | data formatting | bytes 32768
Async XLA Ops:
  1.9 1.0 %copy-start = (bf16[64,4096]{1,0:T(8,128)(2,1)S(1)}, bf16[64,4096]{1,0:T(8,128)(2,1)}, u32[]{:S(2)}) copy-start(bf16[64,4096]{1,0:T(8,128)(2,1)} %src_feat.1) | copy-start | bytes 1572868
  3.0 0.9 %copy-start.1 = (bf16[64,2048]{1,0:T(8,128)(2,1)S(1)}, bf16[64,2048]{1,0:T(8,128)(2,1)}, u32[]{:S(2)}) copy-start(bf16[64,2048]{1,0:T(8,128)(2,1)} %tgt_feat.1) | copy-start | bytes 786436
  3.9 0.8 %copy-start.2 = (f32[3,4096]{1,0:T(4,128)S(1)}, f32[3,4096]{1,0:T(4,128)}, u32[]{:S(2)}) copy-start(f32[3,4096]{1,0:T(4,128)} %src_pos.3) | copy-start | bytes 147460
  4.8 0.8 %copy-start.3 = (f32[3,4096]{1,0:T(4,128)S(1)}, f32[3,4096]{1,0:T(4,128)}, u32[]{:S(2)}) copy-start(f32[3,4096]{1,0:T(4,128)} %disp.3) | copy-start | bytes 147460
  5.6 0.8 %copy-start.5 = (f32[3,2048]{1,0:T(4,128)S(1)}, f32[3,2048]{1,0:T(4,128)}, u32[]{:S(2)}) copy-start(f32[3,2048]{1,0:T(4,128)} %tgt_pos.1) | copy-start | bytes 73732
  6.4 0.7 %copy-start.6 = (s32[4096]{0:T(1024)S(1)}, s32[4096]{0:T(1024)}, u32[]{:S(2)}) copy-start(s32[4096]{0:T(1024)} %param.15) | copy-start | bytes 49156
  7.1 14.1 %copy-start.4 = (s32[8,4096]{1,0:T(8,128)S(1)}, s32[8,4096]{1,0:T(8,128)}, u32[]{:S(2)}) copy-start(s32[8,4096]{1,0:T(8,128)} %edges.1) | copy-start | bytes 393220
where the time goes:
time: 54.3 us; the launch traced here: 53.9 us
  Pallas kernels  45.5 us (84%)
  local copies, waits for them, and re-layouts  6.38 us (12%)
  between operations  1.96 us (4%)
    pallas_call x1, Pallas kernels, on_device(): pl.pallas_call(sweep_kernel, out_shape=(jax.ShapeDtypeStruct((3, points),...  31.4 us
    pallas_call x1, Pallas kernels, on_device(): pl.pallas_call(posterior_kernel, out_shape=jax.ShapeDtypeStruct((half //...  14.1 us
    unnamed x16, local copies, waits for them, and re-layouts  6.38 us

commit v1 on v0

v1 whole, which is shorter than its diff:
```python
import math

import jax
import jax.numpy as jnp
from jax import lax
from jax.experimental import pallas as pl
from jax.experimental.pallas import tpu as pltpu
from jax.sharding import PartitionSpec as P

SWEEPS = 4
LANES = 128
BLOCK = 256
REACH = 16

feature_scale = 0.18
tie_gain = 3.0
outlier_level = 1.0
strip_offset = 2.0
kernel_scale = 8.0
coherence = 0.1

EXP2 = feature_scale * math.log2(math.e)
FLOOR = outlier_level / feature_scale
MESH = pl.DeviceIdType.MESH


def split3(value):
    high = value.astype(jnp.bfloat16).astype(jnp.float32)
    rest = value - high
    mid = rest.astype(jnp.bfloat16).astype(jnp.float32)
    return high, mid, rest - mid


def rows8(rows, width):
    at = lax.broadcasted_iota(jnp.int32, (8, width), 0)
    out = jnp.zeros((8, width), jnp.float32)
    for i, row in enumerate(rows):
        out = jnp.where(at == i, jnp.broadcast_to(row, (8, width)), out)
    return out


def cpd_kernel(
    sigma_ref, count_ref, src_feat, tgt_feat, src_pos_in, disp_in, tgt_pos_in, seed_in, edges_in,
    new_disp, mass_out,
    src_pos, disp, tgt_pos, seed, edges, sfeat, tmat, saug, xmat, state,
    parts, pos, edge, geo, geo_in, gaps, kern_own, kern_far, field, field_in, resid, mass_s,
    local_sem, feat_send, feat_recv, part_send, part_recv, geo_send, geo_recv,
    field_send, field_recv, out_send, out_recv,
):
    chans, points = src_feat.shape
    cands = tgt_feat.shape[1]
    tiles = points // LANES
    half = points // 2
    half_tiles = tiles // 2
    wide = half + LANES
    cand_n, strip_n = lax.axis_size("cand"), lax.axis_size("strip")
    s, c, f = lax.axis_index("strip"), lax.axis_index("cand"), lax.axis_index("feat")
    other = 1 - f
    below, above = s > 0, s < strip_n - 1
    own_tiles = half_tiles // cand_n
    rows = own_tiles + 2
    stack = field.shape[1]
    edge_n = edges.shape[0]
    sigma = sigma_ref[0, 0]
    count = count_ref[0, 0]

    def wide_of(part):
        return pl.ds(pl.multiple_of(part * (half - LANES), LANES), wide)

    loads = [
        pltpu.make_async_copy(src, dst, local_sem.at[i])
        for i, (src, dst) in enumerate(
            [
                (tgt_pos_in, tgt_pos),
                (src_pos_in, src_pos),
                (disp_in, disp),
                (seed_in, seed),
                (edges_in, edges),
                (tgt_feat, tmat.at[pl.ds(0, chans)]),
                (src_feat.at[:, wide_of(f)], sfeat.at[pl.ds(0, chans)]),
            ]
        )
    ]
    for load in loads:
        load.start()

    barrier = pltpu.get_barrier_semaphore()
    peers = [(dc, df) for dc in range(cand_n) for df in range(2) if dc or df]

    def peer(dc, df):
        return {"cand": lax.rem(c + dc, cand_n), "feat": lax.rem(f + df, 2)}

    for dc, df in peers:
        pl.semaphore_signal(barrier, inc=1, device_id=peer(dc, df), device_id_type=MESH)

    @pl.when(below)
    def _():
        pl.semaphore_signal(barrier, inc=1, device_id={"strip": s - 1}, device_id_type=MESH)

    @pl.when(above)
    def _():
        pl.semaphore_signal(barrier, inc=1, device_id={"strip": s + 1}, device_id_type=MESH)

    pl.semaphore_wait(barrier, len(peers) + below.astype(jnp.int32) + above.astype(jnp.int32))

    feats = [
        pltpu.make_async_remote_copy(
            src_ref=src, dst_ref=dst, send_sem=feat_send.at[i], recv_sem=feat_recv.at[i],
            device_id={"feat": other}, device_id_type=MESH,
        )
        for i, (src, dst) in enumerate(
            [
                (tgt_feat, tmat.at[pl.ds(chans, chans)]),
                (src_feat.at[:, wide_of(other)], sfeat.at[pl.ds(chans, chans)]),
            ]
        )
    ]
    for copy in feats:
        copy.start()

    def beside(src, dst, send, recv):
        down = pltpu.make_async_remote_copy(
            src_ref=src, dst_ref=dst.at[1], send_sem=send.at[0], recv_sem=recv.at[1],
            device_id={"strip": jnp.maximum(s - 1, 0)}, device_id_type=MESH,
        )
        up = pltpu.make_async_remote_copy(
            src_ref=src, dst_ref=dst.at[0], send_sem=send.at[1], recv_sem=recv.at[0],
            device_id={"strip": jnp.minimum(s + 1, strip_n - 1)}, device_id_type=MESH,
        )

        @pl.when(below)
        def _():
            down.start()

        @pl.when(above)
        def _():
            up.start()

        def finish():
            @pl.when(below)
            def _():
                down.wait_send()
                up.wait_recv()

            @pl.when(above)
            def _():
                up.wait_send()
                down.wait_recv()

        return finish

    @pl.when(jnp.logical_not(below))
    def _():
        geo_in[0] = jnp.zeros(geo_in.shape[1:], jnp.float32)
        for k in range(SWEEPS + 1):
            field_in[k, 0] = jnp.zeros(field_in.shape[2:], jnp.float32)

    @pl.when(jnp.logical_not(above))
    def _():
        geo_in[1] = jnp.zeros(geo_in.shape[1:], jnp.float32)
        for k in range(SWEEPS + 1):
            field_in[k, 1] = jnp.zeros(field_in.shape[2:], jnp.float32)

    inv = 1.0 / (sigma * feature_scale)
    loads[0].wait()
    x = [tgt_pos[i : i + 1, :] for i in range(3)]
    xx = x[0] * x[0] + x[1] * x[1] + x[2] * x[2]
    one = jnp.ones((1, cands), jnp.float32)
    high, mid, low = split3(rows8(x + [xx * (-0.5 * inv), one], cands))
    tmat[2 * chans : 2 * chans + 48] = jnp.concatenate(
        [high, high, mid, mid, high, low], axis=0
    ).astype(jnp.bfloat16)
    high, mid, low = split3(rows8(x + [one], cands))
    columns = jnp.concatenate(
        [high, mid, low, jnp.zeros((LANES - 24, cands), jnp.float32)], axis=0
    )
    xmat[...] = jnp.transpose(columns).astype(jnp.bfloat16)
    for load in loads[1:5]:
        load.wait()

    first = f * half_tiles + c * own_tiles - 1
    for r in range(rows):
        tile = jnp.clip(first + r, 0, tiles - 1)
        span = pl.ds(pl.multiple_of(tile * LANES, LANES), LANES)
        here, moved, names = src_pos[:, span], disp[:, span], edges[:, span]
        for j in range(3):
            geo[j * rows + r : j * rows + r + 1, :] = here[j : j + 1]
            pos[j * rows + r : j * rows + r + 1, :] = moved[j : j + 1]
            edge[:, j * rows + r, :] = names
    rest = stack - 3 * rows
    geo[3 * rows :, :] = jnp.full((rest, LANES), count.astype(jnp.float32))
    pos[3 * rows :, :] = jnp.zeros((rest, LANES), jnp.float32)
    for k in range(edge_n):
        edge[k, 3 * rows :, :] = jnp.zeros((rest, LANES), jnp.int32)
    finish_geo = beside(geo, geo_in, geo_send, geo_recv)

    mine = wide_of(f)
    z = [src_pos[i : i + 1, mine] + disp[i : i + 1, mine] for i in range(3)]
    zz = z[0] * z[0] + z[1] * z[1] + z[2] * z[2]
    ones = jnp.ones((1, wide), jnp.float32)
    high, mid, low = split3(rows8([v * inv for v in z] + [ones, zz * (-0.5 * inv)], wide))
    saug[...] = jnp.concatenate([high, mid, high, mid, low, high], axis=0).astype(jnp.bfloat16)
    offset = c * cands
    state[0] = jnp.zeros((8, LANES), jnp.float32)
    state[half_tiles + 1] = jnp.zeros((8, LANES), jnp.float32)
    for load in loads[5:]:
        load.wait()
    for copy in feats:
        copy.wait()

    def block(tile, count_of):
        size = count_of * LANES
        span = pl.ds(pl.multiple_of(tile * LANES, LANES), size)
        lhs = jnp.concatenate([sfeat[:, span], saug[:, span]], axis=0)
        score = lax.dot_general(
            lhs, tmat[...], (((0,), (0,)), ((), ())), preferred_element_type=jnp.float32
        )
        seeds = []
        for i in range(count_of):
            row = seed[pl.ds(f * (half_tiles - 1) + tile + i, 1), :] - offset
            seeds.append(jnp.transpose(jnp.broadcast_to(row.astype(jnp.float32), (LANES, LANES))))
        seeds = jnp.concatenate(seeds, axis=0)
        lane = lax.broadcasted_iota(jnp.int32, (size, LANES), 1).astype(jnp.float32)
        pieces = []
        for t in range(cands // LANES):
            piece = score[:, t * LANES : (t + 1) * LANES]
            tie = jnp.where(seeds == lane + float(t * LANES), tie_gain / feature_scale, 0.0)
            pieces.append(piece + tie)
        best = pieces[0]
        for piece in pieces[1:]:
            best = jnp.maximum(best, piece)
        peak = jnp.maximum(jnp.max(best, axis=1, keepdims=True), FLOOR)
        weight = jnp.concatenate([jnp.exp2((piece - peak) * EXP2) for piece in pieces], axis=1)
        high = weight.astype(jnp.bfloat16)
        low = (weight - high.astype(jnp.float32)).astype(jnp.bfloat16)
        sums = jnp.dot(high, xmat[...], preferred_element_type=jnp.float32)
        sums = sums + jnp.dot(low, xmat[...], preferred_element_type=jnp.float32)
        at = lax.broadcasted_iota(jnp.int32, (size, LANES), 1)
        sums = jnp.where(at == 28, jnp.broadcast_to(peak, (size, LANES)), sums)
        for i in range(count_of):
            turned = jnp.transpose(sums[i * LANES : (i + 1) * LANES])
            state[other + tile + i] = turned[0:8] + turned[8:16] + turned[16:24] + turned[24:32]

    per = BLOCK // LANES

    def full(index, carry):
        block(index * per, per)
        return carry

    lax.fori_loop(0, (half_tiles + 1) // per, full, 0)
    if (half_tiles + 1) % per:
        block((half_tiles + 1) // per * per, (half_tiles + 1) % per)

    part_copies = []
    for dc in range(1, cand_n):
        to = lax.rem(c + dc, cand_n)
        copy = pltpu.make_async_remote_copy(
            src_ref=state.at[pl.ds(to * own_tiles, rows)], dst_ref=parts.at[c],
            send_sem=part_send.at[dc - 1], recv_sem=part_recv.at[dc - 1],
            device_id={"cand": to}, device_id_type=MESH,
        )
        copy.start()
        part_copies.append(copy)
    parts[c] = state[pl.ds(c * own_tiles, rows)]

    lane = lax.broadcasted_iota(jnp.int32, (stack, LANES), 1)
    row = lax.broadcasted_iota(jnp.int32, (stack, LANES), 0)
    coord = (row >= rows).astype(jnp.int32) + (row >= 2 * rows).astype(jnp.int32)
    row = first + row - coord * rows

    def pair(array):
        ends = jnp.where(lane < LANES // 2, pltpu.roll(array, stack - 1, 0), pltpu.roll(array, 1, 0))
        return array, ends

    def pick(arrays, at, inside):
        return jnp.where(
            inside,
            jnp.take_along_axis(arrays[0], at, axis=1, mode="promise_in_bounds"),
            jnp.take_along_axis(arrays[1], at, axis=1, mode="promise_in_bounds"),
        )

    def decode(k):
        e = edge[k]
        segment = (e >= points).astype(jnp.int32) + (e >= 2 * points).astype(jnp.int32)
        local = e - segment * points
        at = lax.bitwise_and(local, LANES - 1)
        return segment, local, at, lax.shift_right_logical(local, 7) == row

    slot = row * LANES + lane
    live = jnp.logical_and(jnp.logical_and(slot >= 0, slot < points), slot < count)
    finish_geo()
    counts = [geo_in[0, 3 * rows : 3 * rows + 1, :], geo[3 * rows : 3 * rows + 1, :],
              geo_in[1, 3 * rows : 3 * rows + 1, :]]
    sources = [pair(geo_in[0]), pair(geo[...]), pair(geo_in[1])]
    for k in range(edge_n):
        segment, local, at, inside = decode(k)
        near, limit = (
            jnp.where(segment == 1, b, jnp.where(segment == 0, a, d))
            for a, b, d in (
                [pick(source, at, inside) for source in sources],
                [jnp.broadcast_to(n, (stack, LANES)) for n in counts],
            )
        )
        step = jnp.where(coord == 0, strip_offset * (segment - 1).astype(jnp.float32), 0.0)
        gap = geo[...] - near - step
        gaps[k] = gap * gap
        weight = jnp.where(
            jnp.logical_and(live, local.astype(jnp.float32) < limit), 1.0 / edge_n, 0.0
        )
        kern_own[k] = jnp.where(segment == 1, weight, 0.0)
        kern_far[k] = jnp.where(segment == 1, 0.0, weight)
    for k in range(edge_n):
        squared = (
            gaps[k, 0:rows] + gaps[k, rows : 2 * rows] + gaps[k, 2 * rows : 3 * rows]
        )
        value = jnp.exp(squared * (-0.5 / kernel_scale))
        for j in range(3):
            gaps[k, j * rows : (j + 1) * rows] = value
        kern_own[k] = kern_own[k] * gaps[k]
        kern_far[k] = kern_far[k] * gaps[k]

    resid[...] = jnp.zeros((stack, LANES), jnp.float32)
    mass_s[...] = jnp.zeros((stack, LANES), jnp.float32)
    for copy in part_copies:
        copy.wait()
    peaks = [parts[i, :, 4, :] for i in range(cand_n)]
    peak = peaks[0]
    for one_peak in peaks[1:]:
        peak = jnp.maximum(peak, one_peak)
    sums = [jnp.zeros((rows, LANES), jnp.float32) for _ in range(4)]
    for i in range(cand_n):
        scale = jnp.exp2((peaks[i] - peak) * EXP2)
        sums = [sums[j] + parts[i, :, j, :] * scale for j in range(4)]
    denom = sums[3] + jnp.exp2((FLOOR - peak) * EXP2)
    on = live[0:rows].astype(jnp.float32)
    share = on / denom
    for j in range(3):
        resid[j * rows : (j + 1) * rows] = sums[j] * share
        mass_s[j * rows : (j + 1) * rows] = sums[3] * share
    mass = mass_s[...]
    resid[...] = resid[...] - mass * (geo[...] + pos[...])
    inverse = 1.0 / (mass + coherence * sigma)
    field[0] = resid[...] * inverse

    for step in range(SWEEPS + 1):
        finish = beside(field.at[step], field_in.at[step], field_send.at[step], field_recv.at[step])
        own = pair(field[step])
        acc = jnp.zeros((stack, LANES), jnp.float32)
        for k in range(edge_n):
            _, _, at, inside = decode(k)
            acc = acc + kern_own[k] * pick(own, at, inside)
        finish()
        low = pair(field_in[step, 0])
        high = pair(field_in[step, 1])
        for k in range(edge_n):
            segment, _, at, inside = decode(k)
            acc = acc + kern_far[k] * jnp.where(
                segment == 0, pick(low, at, inside), pick(high, at, inside)
            )
        if step < SWEEPS:
            field[step + 1] = (resid[...] - mass_s[...] * acc) * inverse
        else:
            pos[...] = pos[...] + field[step] + acc

    for r in range(own_tiles):
        span = pl.ds(pl.multiple_of((first + 1 + r) * LANES, LANES), LANES)
        for j in range(3):
            new_disp[j : j + 1, span] = pos[j * rows + r + 1 : j * rows + r + 2, :]
        mass_out[0:1, span] = mass_s[r + 1 : r + 2, :]
    span = pl.ds(pl.multiple_of((first + 1) * LANES, LANES), own_tiles * LANES)
    outs = []
    for i, (dc, df) in enumerate(peers):
        for j, ref in enumerate((new_disp, mass_out)):
            copy = pltpu.make_async_remote_copy(
                src_ref=ref.at[:, span], dst_ref=ref.at[:, span],
                send_sem=out_send.at[i, j], recv_sem=out_recv.at[i, j],
                device_id=peer(dc, df), device_id_type=MESH,
            )
            copy.start()
            outs.append(copy)
    for copy in outs:
        copy.wait()


def on_device(
    src_pos, src_feat, tgt_pos, tgt_feat, displacement, sigma_sq, seed_target, counts, edges
):
    chans, points = src_feat.shape
    cands = tgt_pos.shape[1]
    tiles = points // LANES
    wide = points // 2 + LANES
    edge_n = edges.shape[0]
    cand_n = lax.axis_size("cand")
    rows = tiles // (2 * cand_n) + 2
    assert REACH * (SWEEPS + 1) <= LANES
    grid = (-(-(3 * rows + 1) // 8) * 8, LANES)
    vmem = pl.BlockSpec(memory_space=pltpu.VMEM)
    smem = pl.BlockSpec(memory_space=pltpu.SMEM)
    hbm = pl.BlockSpec(memory_space=pltpu.HBM)
    f32, bf16, i32 = jnp.float32, jnp.bfloat16, jnp.int32
    dma = pltpu.SemaphoreType.DMA
    new_disp, mass = pl.pallas_call(
        cpd_kernel,
        out_shape=(
            jax.ShapeDtypeStruct((3, points), f32),
            jax.ShapeDtypeStruct((1, points), f32),
        ),
        in_specs=[smem, smem] + [hbm] * 7,
        out_specs=(vmem, vmem),
        scratch_shapes=[
            pltpu.VMEM((3, points), f32),
            pltpu.VMEM((3, points), f32),
            pltpu.VMEM((3, cands), f32),
            pltpu.VMEM((tiles, LANES), i32),
            pltpu.VMEM((edge_n, points), i32),
            pltpu.VMEM((2 * chans, wide), bf16),
            pltpu.VMEM((2 * chans + 48, cands), bf16),
            pltpu.VMEM((48, wide), bf16),
            pltpu.VMEM((cands, LANES), bf16),
            pltpu.VMEM((tiles // 2 + 2, 8, LANES), f32),
            pltpu.VMEM((cand_n, rows, 8, LANES), f32),
            pltpu.VMEM(grid, f32),
            pltpu.VMEM((edge_n,) + grid, i32),
            pltpu.VMEM(grid, f32),
            pltpu.VMEM((2,) + grid, f32),
            pltpu.VMEM((edge_n,) + grid, f32),
            pltpu.VMEM((edge_n,) + grid, f32),
            pltpu.VMEM((edge_n,) + grid, f32),
            pltpu.VMEM((SWEEPS + 1,) + grid, f32),
            pltpu.VMEM((SWEEPS + 1, 2) + grid, f32),
            pltpu.VMEM(grid, f32),
            pltpu.VMEM(grid, f32),
            dma((7,)),
            dma((2,)),
            dma((2,)),
            dma((cand_n,)),
            dma((cand_n,)),
            dma((2,)),
            dma((2,)),
            dma((SWEEPS + 1, 2)),
            dma((SWEEPS + 1, 2)),
            dma((2 * cand_n - 1, 2)),
            dma((2 * cand_n - 1, 2)),
        ],
        compiler_params=pltpu.CompilerParams(
            collective_id=0, has_side_effects=True, vmem_limit_bytes=48 << 20
        ),
    )(
        sigma_sq.reshape(1, 1), counts.reshape(1, 1), src_feat, tgt_feat, src_pos, displacement,
        tgt_pos, seed_target.reshape(tiles, LANES), edges,
    )
    return (new_disp, mass.reshape(points))


def solution(mesh):
    in_specs = (
        P(None, ("groups", "strip")),
        P("feat", ("groups", "strip")),
        P(None, ("groups", "strip", "cand")),
        P("feat", ("groups", "strip", "cand")),
        P(None, ("groups", "strip")),
        P(("groups", "strip")),
        P(("groups", "strip")),
        P(("groups", "strip")),
        P(None, ("groups", "strip")),
    )
    out_specs = (P(None, ("groups", "strip")), P(("groups", "strip")))
    return jax.shard_map(
        on_device, mesh=mesh, in_specs=in_specs, out_specs=out_specs, check_vma=False
    )
```

time: 54.3 us -> 51.5 us (0.948)
  Pallas kernels: 45.5 us -> 41.9 us
  local copies, waits for them, and re-layouts: 6.38 us -> 7.28 us
    pallas_call x2 -> x1, Pallas kernels: 45.5 us -> 41.9 us  [on_device(): pl.pallas_call(cpd_kernel, out_shape=(jax.ShapeDtypeStruct((3, points), f...]
    unnamed x16, local copies, waits for them, and re-layouts: 6.38 us -> 7.28 us
where the time goes in v1:
time: 51.5 us; the launch traced here: 51.1 us
  Pallas kernels  41.9 us (81%)
  local copies, waits for them, and re-layouts  7.28 us (14%)
  between operations  1.95 us (4%)
    pallas_call x1, Pallas kernels, on_device(): pl.pallas_call(cpd_kernel, out_shape=(jax.ShapeDtypeStruct((3, points), f...  41.9 us
    unnamed x16, local copies, waits for them, and re-layouts  7.28 us

profile of v1, /device:TPU:0, one launch (start us, length us, event | category | flops | bytes accessed | tf_op | source)
XLA Modules:
  0.0 51.1 jit_solution(13181679890203549474)
XLA Ops:
  1.9 0.0 copy-start
  1.9 1.0 %copy-done = bf16[64,4096]{1,0:T(8,128)(2,1)S(1)} copy-done((bf16[64,4096]{1,0:T(8,128)(2,1)S(1)}, bf16[64,4096]{1,0:T(8,128)(2,1)}, u32[]{:S(2)}) %copy-start) | copy-done | bytes 524312
  3.0 0.0 copy-start.1
  3.0 0.9 %copy-done.1 = bf16[64,2048]{1,0:T(8,128)(2,1)S(1)} copy-done((bf16[64,2048]{1,0:T(8,128)(2,1)S(1)}, bf16[64,2048]{1,0:T(8,128)(2,1)}, u32[]{:S(2)}) %copy-start.1) | copy-done | bytes 262168
  3.9 0.0 copy-start.2
  3.9 0.9 %copy-done.2 = s32[8,4096]{1,0:T(8,128)S(1)} copy-done((s32[8,4096]{1,0:T(8,128)S(1)}, s32[8,4096]{1,0:T(8,128)}, u32[]{:S(2)}) %copy-start.2) | copy-done | bytes 131096
  4.8 0.0 copy-start.3
  4.8 0.8 %copy-done.3 = f32[3,4096]{1,0:T(4,128)S(1)} copy-done((f32[3,4096]{1,0:T(4,128)S(1)}, f32[3,4096]{1,0:T(4,128)}, u32[]{:S(2)}) %copy-start.3) | copy-done | bytes 49176
  5.7 0.0 copy-start.4
  5.7 0.8 %copy-done.4 = f32[3,4096]{1,0:T(4,128)S(1)} copy-done((f32[3,4096]{1,0:T(4,128)S(1)}, f32[3,4096]{1,0:T(4,128)}, u32[]{:S(2)}) %copy-start.4) | copy-done | bytes 49176
  6.5 0.0 copy-start.5
  6.5 0.8 %copy-done.5 = f32[3,2048]{1,0:T(4,128)S(1)} copy-done((f32[3,2048]{1,0:T(4,128)S(1)}, f32[3,2048]{1,0:T(4,128)}, u32[]{:S(2)}) %copy-start.5) | copy-done | bytes 24600
  7.3 0.0 copy-start.6
  7.3 0.7 %copy-done.6 = s32[4096]{0:T(1024)S(1)} copy-done((s32[4096]{0:T(1024)S(1)}, s32[4096]{0:T(1024)}, u32[]{:S(2)}) %copy-start.6) | copy-done | bytes 16408
  8.0 41.9 %shard_map.104 = (f32[3,4096]{1,0:T(4,128)S(1)}, f32[1,4096]{1,0:T(1,128)S(1)}) custom-call(f32[1,1]{1,0:T(1,128)} %bitcast.4.sigma_ref, s32[1,1]{1,0:T(1,128)} %bitcast.5.count_ref, bf16[64,4096]{1,0:T(8,128)(2,1)S(1)} %copy-done, bf16[64,2048]{1,0:T(8,128)(2,1)S(1)} %copy-done.1, f32[3,4096]{1,0:T(4,128)S(1)} %copy-done.3, f32[3,4096]{1,0:T(4,128)S(1)} %copy-done.4, ...), custom_call_target="tpu_custom_call" | custom-call | tf_op jit(solution)/shard_map/pallas_call | solution.py:402
  49.9 0.6 %copy.15 = f32[3,4096]{1,0:T(4,128)} copy(f32[3,4096]{1,0:T(4,128)S(1)} %get-tuple-element.8) | data formatting | bytes 98304
  50.5 0.6 %copy.16 = f32[4096]{0:T(1024)} copy(f32[4096]{0:T(1024)S(1)} %bitcast.7) | data formatting | bytes 32768
Async XLA Ops:
  1.9 1.0 %copy-start = (bf16[64,4096]{1,0:T(8,128)(2,1)S(1)}, bf16[64,4096]{1,0:T(8,128)(2,1)}, u32[]{:S(2)}) copy-start(bf16[64,4096]{1,0:T(8,128)(2,1)} %src_feat.1) | copy-start | bytes 1572868
  3.0 0.9 %copy-start.1 = (bf16[64,2048]{1,0:T(8,128)(2,1)S(1)}, bf16[64,2048]{1,0:T(8,128)(2,1)}, u32[]{:S(2)}) copy-start(bf16[64,2048]{1,0:T(8,128)(2,1)} %tgt_feat.1) | copy-start | bytes 786436
  3.9 0.9 %copy-start.2 = (s32[8,4096]{1,0:T(8,128)S(1)}, s32[8,4096]{1,0:T(8,128)}, u32[]{:S(2)}) copy-start(s32[8,4096]{1,0:T(8,128)} %edges_in.1) | copy-start | bytes 393220
  4.8 0.8 %copy-start.3 = (f32[3,4096]{1,0:T(4,128)S(1)}, f32[3,4096]{1,0:T(4,128)}, u32[]{:S(2)}) copy-start(f32[3,4096]{1,0:T(4,128)} %src_pos_in.1) | copy-start | bytes 147460
  5.7 0.8 %copy-start.4 = (f32[3,4096]{1,0:T(4,128)S(1)}, f32[3,4096]{1,0:T(4,128)}, u32[]{:S(2)}) copy-start(f32[3,4096]{1,0:T(4,128)} %disp_in.1) | copy-start | bytes 147460
  6.5 0.8 %copy-start.5 = (f32[3,2048]{1,0:T(4,128)S(1)}, f32[3,2048]{1,0:T(4,128)}, u32[]{:S(2)}) copy-start(f32[3,2048]{1,0:T(4,128)} %tgt_pos_in.1) | copy-start | bytes 73732
  7.3 0.7 %copy-start.6 = (s32[4096]{0:T(1024)S(1)}, s32[4096]{0:T(1024)}, u32[]{:S(2)}) copy-start(s32[4096]{0:T(1024)} %param.15) | copy-start | bytes 49156

commit v2 on v1

--- a/solution.py
+++ b/solution.py
@@ -43,7 +43,7 @@
     sigma_ref, count_ref, src_feat, tgt_feat, src_pos_in, disp_in, tgt_pos_in, seed_in, edges_in,
     new_disp, mass_out,
     src_pos, disp, tgt_pos, seed, edges, sfeat, tmat, saug, xmat, state,
-    parts, pos, edge, geo, geo_in, gaps, kern_own, kern_far, field, field_in, resid, mass_s,
+    parts, pos, edge, geo, geo_in, gaps, kern_own, kern_far, field, field_in, resid, mass_s, whole, scores,
     local_sem, feat_send, feat_recv, part_send, part_recv, geo_send, geo_recv,
     field_send, field_recv, out_send, out_recv,
 ):
@@ -208,13 +208,15 @@
     for copy in feats:
         copy.wait()
 
-    def block(tile, count_of):
+    def products(tile, into):
+        span = pl.ds(pl.multiple_of(tile * LANES, LANES), BLOCK)
+        lhs = jnp.concatenate([sfeat[:, span], saug[:, span]], axis=0)
+        scores[into] = lax.dot_general(
+            lhs, tmat[...], (((0,), (0,)), ((), ())), preferred_element_type=jnp.float32
+        )
+
+    def block(tile, count_of, held):
         size = count_of * LANES
-        span = pl.ds(pl.multiple_of(tile * LANES, LANES), size)
-        lhs = jnp.concatenate([sfeat[:, span], saug[:, span]], axis=0)
-        score = lax.dot_general(
-            lhs, tmat[...], (((0,), (0,)), ((), ())), preferred_element_type=jnp.float32
-        )
         seeds = []
         for i in range(count_of):
             row = seed[pl.ds(f * (half_tiles - 1) + tile + i, 1), :] - offset
@@ -223,7 +225,7 @@
         lane = lax.broadcasted_iota(jnp.int32, (size, LANES), 1).astype(jnp.float32)
         pieces = []
         for t in range(cands // LANES):
-            piece = score[:, t * LANES : (t + 1) * LANES]
+            piece = scores[held, BLOCK - size :, t * LANES : (t + 1) * LANES]
             tie = jnp.where(seeds == lane + float(t * LANES), tie_gain / feature_scale, 0.0)
             pieces.append(piece + tie)
         best = pieces[0]
@@ -243,13 +245,20 @@
 
     per = BLOCK // LANES
 
+    last = half_tiles + 1 - per
+
     def full(index, carry):
-        block(index * per, per)
+        tile = index * 2 * per
+        products(tile + per, 1)
+        block(tile, per, 0)
+        products(jnp.minimum(tile + 2 * per, last), 0)
+        block(tile + per, per, 1)
         return carry
 
-    lax.fori_loop(0, (half_tiles + 1) // per, full, 0)
-    if (half_tiles + 1) % per:
-        block((half_tiles + 1) // per * per, (half_tiles + 1) % per)
+    assert half_tiles % (2 * per) == 0
+    products(0, 0)
+    lax.fori_loop(0, half_tiles // (2 * per), full, 0)
+    block(half_tiles, 1, 0)
 
     part_copies = []
     for dc in range(1, cand_n):
@@ -365,21 +374,22 @@
     for r in range(own_tiles):
         span = pl.ds(pl.multiple_of((first + 1 + r) * LANES, LANES), LANES)
         for j in range(3):
-            new_disp[j : j + 1, span] = pos[j * rows + r + 1 : j * rows + r + 2, :]
-        mass_out[0:1, span] = mass_s[r + 1 : r + 2, :]
+            whole[j : j + 1, span] = pos[j * rows + r + 1 : j * rows + r + 2, :]
+        whole[3:4, span] = mass_s[r + 1 : r + 2, :]
     span = pl.ds(pl.multiple_of((first + 1) * LANES, LANES), own_tiles * LANES)
     outs = []
     for i, (dc, df) in enumerate(peers):
-        for j, ref in enumerate((new_disp, mass_out)):
-            copy = pltpu.make_async_remote_copy(
-                src_ref=ref.at[:, span], dst_ref=ref.at[:, span],
-                send_sem=out_send.at[i, j], recv_sem=out_recv.at[i, j],
-                device_id=peer(dc, df), device_id_type=MESH,
-            )
-            copy.start()
-            outs.append(copy)
+        copy = pltpu.make_async_remote_copy(
+            src_ref=whole.at[:, span], dst_ref=whole.at[:, span],
+            send_sem=out_send.at[i], recv_sem=out_recv.at[i],
+            device_id=peer(dc, df), device_id_type=MESH,
+        )
+        copy.start()
+        outs.append(copy)
     for copy in outs:
         copy.wait()
+    new_disp[...] = whole[0:3]
+    mass_out[...] = whole[3:4]
 
 
 def on_device(
@@ -430,6 +440,8 @@
             pltpu.VMEM((SWEEPS + 1, 2) + grid, f32),
             pltpu.VMEM(grid, f32),
             pltpu.VMEM(grid, f32),
+            pltpu.VMEM((4, points), f32),
+            pltpu.VMEM((2, BLOCK, cands), f32),
             dma((7,)),
             dma((2,)),
             dma((2,)),
@@ -439,11 +451,11 @@
             dma((2,)),
             dma((SWEEPS + 1, 2)),
             dma((SWEEPS + 1, 2)),
-            dma((2 * cand_n - 1, 2)),
-            dma((2 * cand_n - 1, 2)),
+            dma((2 * cand_n - 1,)),
+            dma((2 * cand_n - 1,)),
         ],
         compiler_params=pltpu.CompilerParams(
-            collective_id=0, has_side_effects=True, vmem_limit_bytes=48 << 20
+            collective_id=0, has_side_effects=True, vmem_limit_bytes=63 << 20
         ),
     )(
         sigma_sq.reshape(1, 1), counts.reshape(1, 1), src_feat, tgt_feat, src_pos, displacement,

time: 51.5 us -> 45.1 us (0.88)
  local copies, waits for them, and re-layouts: 7.28 us -> 2.1 us
  Pallas kernels: 41.9 us -> 40.9 us
    unnamed x16 -> x4, local copies, waits for them, and re-layouts: 7.28 us -> 2.1 us
    pallas_call x1, Pallas kernels: 41.9 us -> 40.9 us  [on_device(): pl.pallas_call(cpd_kernel, out_shape=(jax.ShapeDtypeStruct((3, points), f...]
where the time goes in v2:
time: 45.1 us; the launch traced here: 44.9 us
  Pallas kernels  40.9 us (91%)
  local copies, waits for them, and re-layouts  2.1 us (5%)
  between operations  1.94 us (4%)
    pallas_call x1, Pallas kernels, on_device(): pl.pallas_call(cpd_kernel, out_shape=(jax.ShapeDtypeStruct((3, points), f...  40.9 us
    unnamed x4, local copies, waits for them, and re-layouts  2.1 us

profile of v2, /device:TPU:0, one launch (start us, length us, event | category | flops | bytes accessed | tf_op | source)
XLA Modules:
  0.0 44.9 jit_solution(11471704550410959904)
XLA Ops:
  1.9 40.9 %shard_map.104 = (f32[3,4096]{1,0:T(4,128)}, f32[1,4096]{1,0:T(1,128)}) custom-call(f32[1,1]{1,0:T(1,128)} %bitcast.4.sigma_ref, s32[1,1]{1,0:T(1,128)} %bitcast.5.count_ref, bf16[64,4096]{1,0:T(8,128)(2,1)} %src_feat.1, bf16[64,2048]{1,0:T(8,128)(2,1)} %tgt_feat.1, f32[3,4096]{1,0:T(4,128)} %src_pos_in.1, f32[3,4096]{1,0:T(4,128)} %disp_in.1, ...), custom_call_target="tpu_custom_call" | custom-call | tf_op jit(solution)/shard_map/pallas_call | solution.py:412
  42.8 0.0 copy-start
  42.8 1.5 %copy.15 = f32[3,4096]{1,0:T(4,128)} copy(f32[3,4096]{1,0:T(4,128)} %get-tuple-element.8) | data formatting | bytes 98304
  44.3 0.0 copy-done
  44.3 0.6 %copy.16 = f32[4096]{0:T(1024)} copy(f32[4096]{0:T(1024)S(1)} %bitcast.7) | data formatting | bytes 32768
Async XLA Ops:
  42.8 1.5 %copy-start = (f32[1,4096]{1,0:T(1,128)S(1)}, f32[1,4096]{1,0:T(1,128)}, u32[]{:S(2)}) copy-start(f32[1,4096]{1,0:T(1,128)} %get-tuple-element.5) | copy-start | bytes 49156

commit v3 on v2

--- a/solution.py
+++ b/solution.py
@@ -118,6 +118,8 @@
     for copy in feats:
         copy.start()
 
+    sent = []
+
     def beside(src, dst, send, recv):
         down = pltpu.make_async_remote_copy(
             src_ref=src, dst_ref=dst.at[1], send_sem=send.at[0], recv_sem=recv.at[1],
@@ -139,14 +141,13 @@
         def finish():
             @pl.when(below)
             def _():
-                down.wait_send()
                 up.wait_recv()
 
             @pl.when(above)
             def _():
-                up.wait_send()
                 down.wait_recv()
 
+        sent.append((down, up))
         return finish
 
     @pl.when(jnp.logical_not(below))
@@ -206,7 +207,7 @@
     for load in loads[5:]:
         load.wait()
     for copy in feats:
-        copy.wait()
+        copy.wait_recv()
 
     def products(tile, into):
         span = pl.ds(pl.multiple_of(tile * LANES, LANES), BLOCK)
@@ -331,7 +332,7 @@
     resid[...] = jnp.zeros((stack, LANES), jnp.float32)
     mass_s[...] = jnp.zeros((stack, LANES), jnp.float32)
     for copy in part_copies:
-        copy.wait()
+        copy.wait_recv()
     peaks = [parts[i, :, 4, :] for i in range(cand_n)]
     peak = peaks[0]
     for one_peak in peaks[1:]:
@@ -386,6 +387,19 @@
         )
         copy.start()
         outs.append(copy)
+    for copy in feats + part_copies:
+        copy.wait_send()
+
+    @pl.when(below)
+    def _():
+        for down, up in sent:
+            down.wait_send()
+
+    @pl.when(above)
+    def _():
+        for down, up in sent:
+            up.wait_send()
+
     for copy in outs:
         copy.wait()
     new_disp[...] = whole[0:3]

time: 45.1 us -> 45.1 us (level)
  no operation moved by 1% of the time
where the time goes in v3:
time: 45.1 us; the launch traced here: 44.9 us
  Pallas kernels  40.9 us (91%)
  local copies, waits for them, and re-layouts  2.1 us (5%)
  between operations  1.94 us (4%)
    pallas_call x1, Pallas kernels, on_device(): pl.pallas_call(cpd_kernel, out_shape=(jax.ShapeDtypeStruct((3, points), f...  40.9 us
    unnamed x4, local copies, waits for them, and re-layouts  2.1 us

profile of v3, /device:TPU:0, one launch (start us, length us, event | category | flops | bytes accessed | tf_op | source)
XLA Modules:
  0.0 44.9 jit_solution(9767035329563953609)
XLA Ops:
  1.9 40.9 %shard_map.104 = (f32[3,4096]{1,0:T(4,128)}, f32[1,4096]{1,0:T(1,128)}) custom-call(f32[1,1]{1,0:T(1,128)} %bitcast.4.sigma_ref, s32[1,1]{1,0:T(1,128)} %bitcast.5.count_ref, bf16[64,4096]{1,0:T(8,128)(2,1)} %src_feat.1, bf16[64,2048]{1,0:T(8,128)(2,1)} %tgt_feat.1, f32[3,4096]{1,0:T(4,128)} %src_pos_in.1, f32[3,4096]{1,0:T(4,128)} %disp_in.1, ...), custom_call_target="tpu_custom_call" | custom-call | tf_op jit(solution)/shard_map/pallas_call | solution.py:426
  42.8 0.0 copy-start
  42.8 1.5 %copy.15 = f32[3,4096]{1,0:T(4,128)} copy(f32[3,4096]{1,0:T(4,128)} %get-tuple-element.8) | data formatting | bytes 98304
  44.3 0.0 copy-done
  44.3 0.6 %copy.16 = f32[4096]{0:T(1024)} copy(f32[4096]{0:T(1024)S(1)} %bitcast.7) | data formatting | bytes 32768
Async XLA Ops:
  42.8 1.5 %copy-start = (f32[1,4096]{1,0:T(1,128)S(1)}, f32[1,4096]{1,0:T(1,128)}, u32[]{:S(2)}) copy-start(f32[1,4096]{1,0:T(1,128)} %get-tuple-element.5) | copy-start | bytes 49156
